TPU v7x, 32 devices: a whole 2x2x4 slice. The times are simulated.
32 devices in a mesh: ctx: 16 (over z, y, core), fsdp: 2 (over x).
Axes of the slice: x: 2, y: 2, z: 4, core: 2. Of those that a mesh axis runs over, the one named last changes fastest.
Arguments:
- tokens: bfloat16 [2048, 8192], P('ctx', 'fsdp'), may hold values from -6 to 6
- kv_weight: bfloat16 [8192, 512], P('fsdp'), may hold values from -0.0625 to 0.0625
- queries: bfloat16 [2048, 1024], P('ctx', 'fsdp'), may hold values from -360 to 360
- relaxation: float32 [8], P('fsdp'), may hold values from 0.3 to 1
Outputs:
- attention: bfloat16 [2048, 1024], P('ctx', 'fsdp')
All inputs are finite; a program needn't handle non-finite values.
Results may differ from a plain program's by a relative error of at most 0.0075.
The roundings to bfloat16 on the way count: a program that leaves them out, or rounds other values in their place, can miss the bound.
Values may be sent and summed in bfloat16 or wider, within the bound.
A program may use at most 128 MiB of HBM per device.

v0:
```python
import math

import jax
import jax.numpy as jnp
from jax import lax
from jax.sharding import PartitionSpec as P

ITERS = 2


ROPE_BASE = 500000.0
very_low = -1e30


def combined_all(value, axis, join):
    pieces = jax.tree.map(lambda part: lax.all_gather(part, axis), value)
    head = jax.tree.map(lambda part: part[0], pieces)
    tail = jax.tree.map(lambda part: part[1:], pieces)
    running, _ = lax.scan(lambda running, share: (join(running, share), None), head, tail)
    return running


def passed_along(value, axis, steps):
    count = lax.axis_size(axis)
    pairs = [(source, (source + steps) % count) for source in range(count)]
    return lax.ppermute(value, axis, pairs)


def rotate(key_rows, positions):
    half_width = key_rows.shape[-1] // 2
    frequency = jnp.exp(
        jnp.arange(half_width).astype(jnp.float32)
        * (-2.0 * math.log(ROPE_BASE) / key_rows.shape[-1])
    )
    angles = positions[:, None] * frequency[None, :]
    cosine = jnp.cos(angles)
    sine_part = jnp.sin(angles)
    front_half = key_rows[:, :half_width]
    back_half = key_rows[:, half_width:]
    return jnp.concatenate(
        [front_half * cosine - back_half * sine_part, back_half * cosine + front_half * sine_part],
        axis=1,
    )


def score_block(query_heads, key_block):
    score_scale = 1.0 / math.sqrt(key_block.shape[-1])
    return (
        jnp.einsum("hqd,kd->hqk", query_heads, key_block, preferred_element_type=jnp.float32)
        * score_scale
    )


def row_fold(folded, query_heads, key_block, column_block):
    maxima, masses = folded
    shifted = score_block(query_heads, key_block) + column_block[:, None, :]
    new_maxima = jnp.maximum(maxima, jnp.max(shifted, axis=2))
    masses = masses * jnp.exp(maxima - new_maxima) + jnp.sum(
        jnp.exp(shifted - new_maxima[:, :, None]), axis=2
    )
    return (new_maxima, masses)


def column_part(query_heads, key_block, row_pot):
    shifted = score_block(query_heads, key_block) + row_pot[:, :, None]
    maxima = jnp.max(shifted, axis=1)
    masses = jnp.sum(jnp.exp(shifted - maxima[:, None, :]), axis=1)
    return (maxima, masses)


def join_totals(left_pair, right_pair):
    maxima = jnp.maximum(left_pair[0], right_pair[0])
    return (
        maxima,
        left_pair[1] * jnp.exp(left_pair[0] - maxima)
        + right_pair[1] * jnp.exp(right_pair[0] - maxima),
    )


def output_fold(folded, query_heads, key_block, value_block, column_block):
    maxima, masses, numerator = folded
    shifted = score_block(query_heads, key_block) + column_block[:, None, :]
    new_maxima = jnp.maximum(maxima, jnp.max(shifted, axis=2))
    factor = jnp.exp(maxima - new_maxima)
    weights = jnp.exp(shifted - new_maxima[:, :, None])
    masses = masses * factor + jnp.sum(weights, axis=2)
    numerator = numerator * factor[:, :, None] + jnp.einsum(
        "hqk,kd->hqd", weights.astype(jnp.bfloat16), value_block, preferred_element_type=jnp.float32
    )
    return (new_maxima, masses, numerator)


def column_potential(peak_all, mass_all, relax_rates):
    maxima, masses = combined_all((peak_all, mass_all), "ctx", join_totals)
    return -relax_rates[:, None] * (maxima + jnp.log(masses))


def circulate_keys(key_rows, visitor, folded, my_index):
    cycle_size = lax.axis_size("ctx")
    tok_rows = key_rows.shape[0]
    folded = visitor(folded, key_rows, None, my_index * tok_rows)

    def advance(step_index, state_pair):
        held_keys, inner_carry = state_pair
        held_keys = passed_along(held_keys, "ctx", 1)
        first_key = jnp.mod(my_index - step_index, cycle_size) * tok_rows
        return (held_keys, visitor(inner_carry, held_keys, None, first_key))

    return lax.fori_loop(1, cycle_size, advance, (key_rows, folded))[1]


def circulate_pairs(key_rows, value_rows, visitor, folded, my_index):
    cycle_size = lax.axis_size("ctx")
    tok_rows = key_rows.shape[0]
    folded = visitor(folded, key_rows, value_rows, my_index * tok_rows)

    def advance(step_index, state_triple):
        held_keys, held_values, inner_carry = state_triple
        held_keys, held_values = passed_along((held_keys, held_values), "ctx", 1)
        first_key = jnp.mod(my_index - step_index, cycle_size) * tok_rows
        return (held_keys, held_values, visitor(inner_carry, held_keys, held_values, first_key))

    return lax.fori_loop(1, cycle_size, advance, (key_rows, value_rows, folded))[2]


def on_device(tokens, kv_weight, queries, relaxation):
    tok_rows = tokens.shape[0]
    head_count = relaxation.shape[0]
    cycle_size = lax.axis_size("ctx")
    my_index = lax.axis_index("ctx")
    seq_len = tok_rows * cycle_size
    head_slot = kv_weight.shape[1] // lax.axis_size("fsdp")
    half_slot = head_slot // 2
    kv_rows = lax.psum_scatter(
        lax.dot_general(
            kv_weight, tokens, (((0,), (1,)), ((), ())), preferred_element_type=jnp.float32
        ),
        "fsdp",
        scatter_dimension=0,
        tiled=True,
    )
    positions = (my_index * tok_rows + jnp.arange(tok_rows)).astype(jnp.float32)
    key_rows = rotate(kv_rows[:half_slot].T, positions).astype(jnp.bfloat16)
    value_rows = kv_rows[half_slot:].T.astype(jnp.bfloat16)
    query_heads = jnp.transpose(queries.reshape(tok_rows, head_count, half_slot), (1, 0, 2))
    low_state = jnp.full((head_count, tok_rows), very_low, jnp.float32)
    zero_state = jnp.zeros((head_count, tok_rows), jnp.float32)
    blank_rows = jnp.zeros((head_count, seq_len), jnp.float32)
    numer_start = jnp.zeros((head_count, tok_rows, half_slot), jnp.float32)
    column_pot = jnp.zeros((head_count, seq_len), jnp.float32)
    for iteration in range(ITERS):
        current = column_pot

        def row_visit(folded, key_block, value_block, first_key):
            column_block = lax.dynamic_slice_in_dim(current, first_key, key_block.shape[0], 1)
            return row_fold(folded, query_heads, key_block, column_block)

        maxima, masses = circulate_keys(key_rows, row_visit, (low_state, zero_state), my_index)
        row_pot = -relaxation[:, None] * (maxima + jnp.log(masses))

        def column_visit(folded, key_block, value_block, first_key):
            part_peak, part_mass = column_part(query_heads, key_block, row_pot)
            return (
                lax.dynamic_update_slice_in_dim(folded[0], part_peak, first_key, 1),
                lax.dynamic_update_slice_in_dim(folded[1], part_mass, first_key, 1),
            )

        peak_all, mass_all = circulate_keys(
            key_rows, column_visit, (blank_rows, blank_rows), my_index
        )
        column_pot = column_potential(peak_all, mass_all, relaxation)
    final_pot = column_pot

    def output_visit(folded, key_block, value_block, first_key):
        column_block = lax.dynamic_slice_in_dim(final_pot, first_key, key_block.shape[0], 1)
        return output_fold(folded, query_heads, key_block, value_block, column_block)

    maxima, masses, numerator = circulate_pairs(
        key_rows, value_rows, output_visit, (low_state, zero_state, numer_start), my_index
    )
    blended = numerator / masses[:, :, None]
    return (
        jnp.transpose(blended, (1, 0, 2))
        .reshape(tok_rows, head_count * half_slot)
        .astype(jnp.bfloat16)
    )


def solution(mesh):
    placed = (P("ctx", "fsdp"), P("fsdp", None), P("ctx", "fsdp"), P("fsdp"))
    return jax.shard_map(
        on_device, mesh=mesh, in_specs=placed, out_specs=P("ctx", "fsdp"), check_vma=False
    )
```

profile of v0, /device:TPU:0, one launch (start us, length us, event | category | flops | bytes accessed | tf_op | source)
XLA Modules:
  0.0 610.5 jit_solution(7214324194710815978)
XLA Ops:
  12.3 14.3 %reduce-scatter.2.cloned.1.call-done = f32[256,128]{1,0:T(8,128)} async-done(((f32[512,128]{1,0:T(8,128)}), f32[256,128]{1,0:T(8,128)}) %reduce-scatter.2.cloned.1.call-update) | async-done | bytes 131088 | tf_op jit(solution)/shard_map/reduce_scatter | solution.py:134
  28.1 96.4 %while.120 = (s32[]{:T(128)}, bf16[128,128]{1,0:T(8,128)(2,1)S(1)}, f32[4,128]{1,0:T(4,128)S(1)}, f32[4,128]{1,0:T(4,128)S(1)}, bf16[4,128,128]{2,1,0:T(8,128)(2,1)S(1)}, /*index=5*/s32[]{:T(128)}) while((s32[]{:T(128)}, bf16[128,128]{1,0:T(8,128)(2,1)S(1)}, f32[4,128]{1,0:T(4,128)S(1)}, f32[4,128]{1,0:T(4,128)S(1)}, ...), condition=%wide.region_6.7_spmd, body=%wide.region_3.6_spmd.sunk | while | flops 17040384 | bytes 911469 | solution.py:109
  28.2 6.0 collective-permute-done
  34.6 6.0 collective-permute-done
  41.0 6.0 collective-permute-done
  47.5 6.0 collective-permute-done
  53.9 6.0 collective-permute-done
  60.3 6.0 collective-permute-done
  66.7 6.0 collective-permute-done
  73.2 6.0 collective-permute-done
  79.6 6.0 collective-permute-done
  86.0 6.0 collective-permute-done
  92.4 6.0 collective-permute-done
  98.9 6.0 collective-permute-done
  105.3 6.0 collective-permute-done
  111.7 6.0 collective-permute-done
  118.1 6.0 collective-permute-done
  125.0 96.0 %while.121 = (s32[]{:T(128)}, bf16[128,128]{1,0:T(8,128)(2,1)S(1)}, f32[4,2048]{1,0:T(4,128)S(1)}, f32[4,2048]{1,0:T(4,128)S(1)}, bf16[4,128,128]{2,1,0:T(8,128)...) while((s32[]{:T(128)}, bf16[128,128]{1,0:T(8,128)(2,1)S(1)}, ...), condition=%wide.region_12.13_spmd, body=%wide.region_9.12_spmd.sunk | while | flops 17103872 | bytes 901456 | solution.py:109
  125.1 6.0 collective-permute-done.1
  131.5 6.0 collective-permute-done.1
  137.9 6.0 collective-permute-done.1
  144.3 6.0 collective-permute-done.1
  150.8 6.0 collective-permute-done.1
  157.2 6.0 collective-permute-done.1
  163.6 6.0 collective-permute-done.1
  170.0 6.0 collective-permute-done.1
  176.4 6.0 collective-permute-done.1
  182.8 6.0 collective-permute-done.1
  189.2 6.0 collective-permute-done.1
  195.6 6.0 collective-permute-done.1
  202.0 6.0 collective-permute-done.1
  208.4 6.0 collective-permute-done.1
  214.8 6.0 collective-permute-done.1
  221.1 18.7 %all-gather.5 = f32[16,4,2048]{2,1,0:T(4,128)S(1)} all-gather(f32[1,4,2048]{2,1,0:T(4,128)S(1)} %bitcast.125), channel_id=3, replica_groups=mesh['ctx'=16,'fsdp'=2] {'ctx'}, dimensions={0}, use_global_device_ids=true | all-gather | bytes 557056 | tf_op jit(solution)/shard_map/all_gather | solution.py:16
  239.9 21.0 %all-gather.4 = f32[16,4,2048]{2,1,0:T(4,128)S(1)} all-gather(f32[1,4,2048]{2,1,0:T(4,128)S(1)} %bitcast.124), channel_id=2, replica_groups=mesh['ctx'=16,'fsdp'=2] {'ctx'}, dimensions={0}, use_global_device_ids=true | all-gather | bytes 557056 | tf_op jit(solution)/shard_map/all_gather | solution.py:16
  262.3 96.3 %while.123 = (s32[]{:T(128)}, bf16[128,128]{1,0:T(8,128)(2,1)S(1)}, f32[4,128]{1,0:T(4,128)S(1)}, f32[4,128]{1,0:T(4,128)S(1)}, bf16[4,128,128]{2,1,0:T(8,128)(2...) while((s32[]{:T(128)}, bf16[128,128]{1,0:T(8,128)(2,1)S(1)}, ...), condition=%wide.region_20.21_spmd, body=%wide.region_17.20_spmd.sunk | while | flops 17105936 | bytes 917840 | solution.py:109
  359.2 96.0 %while.124 = (s32[]{:T(128)}, bf16[128,128]{1,0:T(8,128)(2,1)S(1)}, f32[4,2048]{1,0:T(4,128)S(1)}, f32[4,2048]{1,0:T(4,128)S(1)}, bf16[4,128,128]{2,1,0:T(8,128)...) while((s32[]{:T(128)}, bf16[128,128]{1,0:T(8,128)(2,1)S(1)}, ...), condition=%wide.region_26.27_spmd, body=%wide.region_23.26_spmd.sunk | while | flops 17103872 | bytes 901456 | solution.py:109
  359.3 6.0 collective-permute-done.3
  365.7 6.0 collective-permute-done.3
  372.1 6.0 collective-permute-done.3
  378.5 6.0 collective-permute-done.3
  384.9 6.0 collective-permute-done.3
  391.3 6.0 collective-permute-done.3
  397.7 6.0 collective-permute-done.3
  404.1 6.0 collective-permute-done.3
  410.5 6.0 collective-permute-done.3
  416.9 6.0 collective-permute-done.3
  455.2 18.7 %all-gather.7 = f32[16,4,2048]{2,1,0:T(4,128)S(1)} all-gather(f32[1,4,2048]{2,1,0:T(4,128)S(1)} %bitcast.123), channel_id=5, replica_groups=mesh['ctx'=16,'fsdp'=2] {'ctx'}, dimensions={0}, use_global_device_ids=true | all-gather | bytes 557056 | tf_op jit(solution)/shard_map/all_gather | solution.py:16
  474.0 21.0 %all-gather.6 = f32[16,4,2048]{2,1,0:T(4,128)S(1)} all-gather(f32[1,4,2048]{2,1,0:T(4,128)S(1)} %bitcast.126), channel_id=4, replica_groups=mesh['ctx'=16,'fsdp'=2] {'ctx'}, dimensions={0}, use_global_device_ids=true | all-gather | bytes 557056 | tf_op jit(solution)/shard_map/all_gather | solution.py:16
  496.9 106.0 %while.126 = (s32[]{:T(128)}, bf16[128,128]{1,0:T(8,128)(2,1)S(1)}, bf16[128,128]{1,0:T(8,128)(2,1)S(1)}, f32[4,128]{1,0:T(4,128)S(1)}, f32[4,128]{1,0:T(4,128)S...) while((s32[]{:T(128)}, bf16[128,128]{1,0:T(8,128)(2,1)S(1)}, ...), condition=%wide.region_34.35_spmd, body=%wide.region_31.34_spmd.sunk | while | flops 34145296 | bytes 1939848 | solution.py:123
  504.1 6.3 %collective-permute-done.4 = bf16[128,128]{1,0:T(8,128)(2,1)S(1)} collective-permute-done((bf16[128,128]{1,0:T(8,128)(2,1)S(1)}, bf16[128,128]{1,0:T(8,128)(2,1)S(1)}, u32[]{:S(2)}, u32[]{:S(2)}) %collective-permute-start.4) | collective-permute-done | bytes 32800 | tf_op jit(solution)/shard_map/while/body/eval_jaxpr/ppermute | solution.py:26
  511.2 6.3 %collective-permute-done.4 = bf16[128,128]{1,0:T(8,128)(2,1)S(1)} collective-permute-done((bf16[128,128]{1,0:T(8,128)(2,1)S(1)}, bf16[128,128]{1,0:T(8,128)(2,1)S(1)}, u32[]{:S(2)}, u32[]{:S(2)}) %collective-permute-start.4) | collective-permute-done | bytes 32800 | tf_op jit(solution)/shard_map/while/body/eval_jaxpr/ppermute | solution.py:26
  518.3 6.3 %collective-permute-done.4 = bf16[128,128]{1,0:T(8,128)(2,1)S(1)} collective-permute-done((bf16[128,128]{1,0:T(8,128)(2,1)S(1)}, bf16[128,128]{1,0:T(8,128)(2,1)S(1)}, u32[]{:S(2)}, u32[]{:S(2)}) %collective-permute-start.4) | collective-permute-done | bytes 32800 | tf_op jit(solution)/shard_map/while/body/eval_jaxpr/ppermute | solution.py:26
  525.3 6.3 %collective-permute-done.4 = bf16[128,128]{1,0:T(8,128)(2,1)S(1)} collective-permute-done((bf16[128,128]{1,0:T(8,128)(2,1)S(1)}, bf16[128,128]{1,0:T(8,128)(2,1)S(1)}, u32[]{:S(2)}, u32[]{:S(2)}) %collective-permute-start.4) | collective-permute-done | bytes 32800 | tf_op jit(solution)/shard_map/while/body/eval_jaxpr/ppermute | solution.py:26
  532.4 6.3 %collective-permute-done.4 = bf16[128,128]{1,0:T(8,128)(2,1)S(1)} collective-permute-done((bf16[128,128]{1,0:T(8,128)(2,1)S(1)}, bf16[128,128]{1,0:T(8,128)(2,1)S(1)}, u32[]{:S(2)}, u32[]{:S(2)}) %collective-permute-start.4) | collective-permute-done | bytes 32800 | tf_op jit(solution)/shard_map/while/body/eval_jaxpr/ppermute | solution.py:26
  539.5 6.3 %collective-permute-done.4 = bf16[128,128]{1,0:T(8,128)(2,1)S(1)} collective-permute-done((bf16[128,128]{1,0:T(8,128)(2,1)S(1)}, bf16[128,128]{1,0:T(8,128)(2,1)S(1)}, u32[]{:S(2)}, u32[]{:S(2)}) %collective-permute-start.4) | collective-permute-done | bytes 32800 | tf_op jit(solution)/shard_map/while/body/eval_jaxpr/ppermute | solution.py:26
  546.5 6.3 %collective-permute-done.4 = bf16[128,128]{1,0:T(8,128)(2,1)S(1)} collective-permute-done((bf16[128,128]{1,0:T(8,128)(2,1)S(1)}, bf16[128,128]{1,0:T(8,128)(2,1)S(1)}, u32[]{:S(2)}, u32[]{:S(2)}) %collective-permute-start.4) | collective-permute-done | bytes 32800 | tf_op jit(solution)/shard_map/while/body/eval_jaxpr/ppermute | solution.py:26
  553.6 6.3 %collective-permute-done.4 = bf16[128,128]{1,0:T(8,128)(2,1)S(1)} collective-permute-done((bf16[128,128]{1,0:T(8,128)(2,1)S(1)}, bf16[128,128]{1,0:T(8,128)(2,1)S(1)}, u32[]{:S(2)}, u32[]{:S(2)}) %collective-permute-start.4) | collective-permute-done | bytes 32800 | tf_op jit(solution)/shard_map/while/body/eval_jaxpr/ppermute | solution.py:26
  560.6 6.3 %collective-permute-done.4 = bf16[128,128]{1,0:T(8,128)(2,1)S(1)} collective-permute-done((bf16[128,128]{1,0:T(8,128)(2,1)S(1)}, bf16[128,128]{1,0:T(8,128)(2,1)S(1)}, u32[]{:S(2)}, u32[]{:S(2)}) %collective-permute-start.4) | collective-permute-done | bytes 32800 | tf_op jit(solution)/shard_map/while/body/eval_jaxpr/ppermute | solution.py:26
  567.7 6.3 %collective-permute-done.4 = bf16[128,128]{1,0:T(8,128)(2,1)S(1)} collective-permute-done((bf16[128,128]{1,0:T(8,128)(2,1)S(1)}, bf16[128,128]{1,0:T(8,128)(2,1)S(1)}, u32[]{:S(2)}, u32[]{:S(2)}) %collective-permute-start.4) | collective-permute-done | bytes 32800 | tf_op jit(solution)/shard_map/while/body/eval_jaxpr/ppermute | solution.py:26
  574.8 6.3 %collective-permute-done.4 = bf16[128,128]{1,0:T(8,128)(2,1)S(1)} collective-permute-done((bf16[128,128]{1,0:T(8,128)(2,1)S(1)}, bf16[128,128]{1,0:T(8,128)(2,1)S(1)}, u32[]{:S(2)}, u32[]{:S(2)}) %collective-permute-start.4) | collective-permute-done | bytes 32800 | tf_op jit(solution)/shard_map/while/body/eval_jaxpr/ppermute | solution.py:26
  581.8 6.3 %collective-permute-done.4 = bf16[128,128]{1,0:T(8,128)(2,1)S(1)} collective-permute-done((bf16[128,128]{1,0:T(8,128)(2,1)S(1)}, bf16[128,128]{1,0:T(8,128)(2,1)S(1)}, u32[]{:S(2)}, u32[]{:S(2)}) %collective-permute-start.4) | collective-permute-done | bytes 32800 | tf_op jit(solution)/shard_map/while/body/eval_jaxpr/ppermute | solution.py:26
  588.9 6.3 %collective-permute-done.4 = bf16[128,128]{1,0:T(8,128)(2,1)S(1)} collective-permute-done((bf16[128,128]{1,0:T(8,128)(2,1)S(1)}, bf16[128,128]{1,0:T(8,128)(2,1)S(1)}, u32[]{:S(2)}, u32[]{:S(2)}) %collective-permute-start.4) | collective-permute-done | bytes 32800 | tf_op jit(solution)/shard_map/while/body/eval_jaxpr/ppermute | solution.py:26
  596.0 6.3 %collective-permute-done.4 = bf16[128,128]{1,0:T(8,128)(2,1)S(1)} collective-permute-done((bf16[128,128]{1,0:T(8,128)(2,1)S(1)}, bf16[128,128]{1,0:T(8,128)(2,1)S(1)}, u32[]{:S(2)}, u32[]{:S(2)}) %collective-permute-start.4) | collective-permute-done | bytes 32800 | tf_op jit(solution)/shard_map/while/body/eval_jaxpr/ppermute | solution.py:26
  (680 shorter events, 171.3 us)
Async XLA Ops:
  6.5 20.1 %reduce-scatter.2.cloned.1.call-start = ((), (), s32[]{:S(2)}) async-start(), calls=%async_computation.1 | async-start | bytes 393216 | tf_op jit(solution)/shard_map/reduce_scatter | solution.py:134
  28.1 6.1 collective-permute-start
  34.6 6.1 collective-permute-start
  41.0 6.1 collective-permute-start
  47.4 6.1 collective-permute-start
  53.8 6.1 collective-permute-start
  60.3 6.1 collective-permute-start
  66.7 6.1 collective-permute-start
  73.1 6.1 collective-permute-start
  79.5 6.1 collective-permute-start
  85.9 6.1 collective-permute-start
  92.4 6.1 collective-permute-start
  98.8 6.1 collective-permute-start
  105.2 6.1 collective-permute-start
  111.6 6.1 collective-permute-start
  118.1 6.1 collective-permute-start
  125.0 6.1 collective-permute-start.1
  131.5 6.1 collective-permute-start.1
  137.9 6.1 collective-permute-start.1
  144.3 6.1 collective-permute-start.1
  182.7 6.1 collective-permute-start.1
  201.9 6.1 collective-permute-start.1
  262.3 6.1 collective-permute-start.2
  275.1 6.1 collective-permute-start.2
  281.6 6.1 collective-permute-start.2
  300.8 6.1 collective-permute-start.2
  307.2 6.1 collective-permute-start.2
  320.1 6.1 collective-permute-start.2
  326.5 6.1 collective-permute-start.2
  345.8 6.1 collective-permute-start.2
  352.2 6.1 collective-permute-start.2
  365.6 6.1 collective-permute-start.3
  372.0 6.1 collective-permute-start.3
  391.2 6.1 collective-permute-start.3
  410.4 6.1 collective-permute-start.3
  496.9 6.8 %collective-permute-start.5 = (bf16[128,128]{1,0:T(8,128)(2,1)S(1)}, bf16[128,128]{1,0:T(8,128)(2,1)S(1)}, u32[]{:S(2)}, u32[]{:S(2)}) collective-permute-start(bf16[128,128]{1,0:T(8,128)(2,1)S(1)} %get-tuple-element.1604), channel_id=1, source_target_pairs={{0,2},{2,4},{4,6},{6,8},{8,10},{10,12},{12,14},{14,16},{16,18},{18... | collective-permute-start | bytes 98312 | tf_op jit(solution)/shard_map/while/body/eval_jaxpr/ppermute | solution.py:26
  504.0 6.8 %collective-permute-start.5 = (bf16[128,128]{1,0:T(8,128)(2,1)S(1)}, bf16[128,128]{1,0:T(8,128)(2,1)S(1)}, u32[]{:S(2)}, u32[]{:S(2)}) collective-permute-start(bf16[128,128]{1,0:T(8,128)(2,1)S(1)} %get-tuple-element.1604), channel_id=1, source_target_pairs={{0,2},{2,4},{4,6},{6,8},{8,10},{10,12},{12,14},{14,16},{16,18},{18... | collective-permute-start | bytes 98312 | tf_op jit(solution)/shard_map/while/body/eval_jaxpr/ppermute | solution.py:26
  504.0 6.4 %collective-permute-start.4 = (bf16[128,128]{1,0:T(8,128)(2,1)S(1)}, bf16[128,128]{1,0:T(8,128)(2,1)S(1)}, u32[]{:S(2)}, u32[]{:S(2)}) collective-permute-start(bf16[128,128]{1,0:T(8,128)(2,1)S(1)} %get-tuple-element.1603), channel_id=1, source_target_pairs={{0,2},{2,4},{4,6},{6,8},{8,10},{10,12},{12,14},{14,16},{16,18},{18... | collective-permute-start | bytes 98312 | tf_op jit(solution)/shard_map/while/body/eval_jaxpr/ppermute | solution.py:26
  511.0 6.8 %collective-permute-start.5 = (bf16[128,128]{1,0:T(8,128)(2,1)S(1)}, bf16[128,128]{1,0:T(8,128)(2,1)S(1)}, u32[]{:S(2)}, u32[]{:S(2)}) collective-permute-start(bf16[128,128]{1,0:T(8,128)(2,1)S(1)} %get-tuple-element.1604), channel_id=1, source_target_pairs={{0,2},{2,4},{4,6},{6,8},{8,10},{10,12},{12,14},{14,16},{16,18},{18... | collective-permute-start | bytes 98312 | tf_op jit(solution)/shard_map/while/body/eval_jaxpr/ppermute | solution.py:26
  511.1 6.4 %collective-permute-start.4 = (bf16[128,128]{1,0:T(8,128)(2,1)S(1)}, bf16[128,128]{1,0:T(8,128)(2,1)S(1)}, u32[]{:S(2)}, u32[]{:S(2)}) collective-permute-start(bf16[128,128]{1,0:T(8,128)(2,1)S(1)} %get-tuple-element.1603), channel_id=1, source_target_pairs={{0,2},{2,4},{4,6},{6,8},{8,10},{10,12},{12,14},{14,16},{16,18},{18... | collective-permute-start | bytes 98312 | tf_op jit(solution)/shard_map/while/body/eval_jaxpr/ppermute | solution.py:26
  518.1 6.8 %collective-permute-start.5 = (bf16[128,128]{1,0:T(8,128)(2,1)S(1)}, bf16[128,128]{1,0:T(8,128)(2,1)S(1)}, u32[]{:S(2)}, u32[]{:S(2)}) collective-permute-start(bf16[128,128]{1,0:T(8,128)(2,1)S(1)} %get-tuple-element.1604), channel_id=1, source_target_pairs={{0,2},{2,4},{4,6},{6,8},{8,10},{10,12},{12,14},{14,16},{16,18},{18... | collective-permute-start | bytes 98312 | tf_op jit(solution)/shard_map/while/body/eval_jaxpr/ppermute | solution.py:26
  518.2 6.4 %collective-permute-start.4 = (bf16[128,128]{1,0:T(8,128)(2,1)S(1)}, bf16[128,128]{1,0:T(8,128)(2,1)S(1)}, u32[]{:S(2)}, u32[]{:S(2)}) collective-permute-start(bf16[128,128]{1,0:T(8,128)(2,1)S(1)} %get-tuple-element.1603), channel_id=1, source_target_pairs={{0,2},{2,4},{4,6},{6,8},{8,10},{10,12},{12,14},{14,16},{16,18},{18... | collective-permute-start | bytes 98312 | tf_op jit(solution)/shard_map/while/body/eval_jaxpr/ppermute | solution.py:26
  525.2 6.8 %collective-permute-start.5 = (bf16[128,128]{1,0:T(8,128)(2,1)S(1)}, bf16[128,128]{1,0:T(8,128)(2,1)S(1)}, u32[]{:S(2)}, u32[]{:S(2)}) collective-permute-start(bf16[128,128]{1,0:T(8,128)(2,1)S(1)} %get-tuple-element.1604), channel_id=1, source_target_pairs={{0,2},{2,4},{4,6},{6,8},{8,10},{10,12},{12,14},{14,16},{16,18},{18... | collective-permute-start | bytes 98312 | tf_op jit(solution)/shard_map/while/body/eval_jaxpr/ppermute | solution.py:26
  525.2 6.4 %collective-permute-start.4 = (bf16[128,128]{1,0:T(8,128)(2,1)S(1)}, bf16[128,128]{1,0:T(8,128)(2,1)S(1)}, u32[]{:S(2)}, u32[]{:S(2)}) collective-permute-start(bf16[128,128]{1,0:T(8,128)(2,1)S(1)} %get-tuple-element.1603), channel_id=1, source_target_pairs={{0,2},{2,4},{4,6},{6,8},{8,10},{10,12},{12,14},{14,16},{16,18},{18... | collective-permute-start | bytes 98312 | tf_op jit(solution)/shard_map/while/body/eval_jaxpr/ppermute | solution.py:26
  532.2 6.8 %collective-permute-start.5 = (bf16[128,128]{1,0:T(8,128)(2,1)S(1)}, bf16[128,128]{1,0:T(8,128)(2,1)S(1)}, u32[]{:S(2)}, u32[]{:S(2)}) collective-permute-start(bf16[128,128]{1,0:T(8,128)(2,1)S(1)} %get-tuple-element.1604), channel_id=1, source_target_pairs={{0,2},{2,4},{4,6},{6,8},{8,10},{10,12},{12,14},{14,16},{16,18},{18... | collective-permute-start | bytes 98312 | tf_op jit(solution)/shard_map/while/body/eval_jaxpr/ppermute | solution.py:26
  532.3 6.4 %collective-permute-start.4 = (bf16[128,128]{1,0:T(8,128)(2,1)S(1)}, bf16[128,128]{1,0:T(8,128)(2,1)S(1)}, u32[]{:S(2)}, u32[]{:S(2)}) collective-permute-start(bf16[128,128]{1,0:T(8,128)(2,1)S(1)} %get-tuple-element.1603), channel_id=1, source_target_pairs={{0,2},{2,4},{4,6},{6,8},{8,10},{10,12},{12,14},{14,16},{16,18},{18... | collective-permute-start | bytes 98312 | tf_op jit(solution)/shard_map/while/body/eval_jaxpr/ppermute | solution.py:26
  539.3 6.8 %collective-permute-start.5 = (bf16[128,128]{1,0:T(8,128)(2,1)S(1)}, bf16[128,128]{1,0:T(8,128)(2,1)S(1)}, u32[]{:S(2)}, u32[]{:S(2)}) collective-permute-start(bf16[128,128]{1,0:T(8,128)(2,1)S(1)} %get-tuple-element.1604), channel_id=1, source_target_pairs={{0,2},{2,4},{4,6},{6,8},{8,10},{10,12},{12,14},{14,16},{16,18},{18... | collective-permute-start | bytes 98312 | tf_op jit(solution)/shard_map/while/body/eval_jaxpr/ppermute | solution.py:26
  539.3 6.4 %collective-permute-start.4 = (bf16[128,128]{1,0:T(8,128)(2,1)S(1)}, bf16[128,128]{1,0:T(8,128)(2,1)S(1)}, u32[]{:S(2)}, u32[]{:S(2)}) collective-permute-start(bf16[128,128]{1,0:T(8,128)(2,1)S(1)} %get-tuple-element.1603), channel_id=1, source_target_pairs={{0,2},{2,4},{4,6},{6,8},{8,10},{10,12},{12,14},{14,16},{16,18},{18... | collective-permute-start | bytes 98312 | tf_op jit(solution)/shard_map/while/body/eval_jaxpr/ppermute | solution.py:26
  546.3 6.8 %collective-permute-start.5 = (bf16[128,128]{1,0:T(8,128)(2,1)S(1)}, bf16[128,128]{1,0:T(8,128)(2,1)S(1)}, u32[]{:S(2)}, u32[]{:S(2)}) collective-permute-start(bf16[128,128]{1,0:T(8,128)(2,1)S(1)} %get-tuple-element.1604), channel_id=1, source_target_pairs={{0,2},{2,4},{4,6},{6,8},{8,10},{10,12},{12,14},{14,16},{16,18},{18... | collective-permute-start | bytes 98312 | tf_op jit(solution)/shard_map/while/body/eval_jaxpr/ppermute | solution.py:26
  546.4 6.4 %collective-permute-start.4 = (bf16[128,128]{1,0:T(8,128)(2,1)S(1)}, bf16[128,128]{1,0:T(8,128)(2,1)S(1)}, u32[]{:S(2)}, u32[]{:S(2)}) collective-permute-start(bf16[128,128]{1,0:T(8,128)(2,1)S(1)} %get-tuple-element.1603), channel_id=1, source_target_pairs={{0,2},{2,4},{4,6},{6,8},{8,10},{10,12},{12,14},{14,16},{16,18},{18... | collective-permute-start | bytes 98312 | tf_op jit(solution)/shard_map/while/body/eval_jaxpr/ppermute | solution.py:26
  553.4 6.8 %collective-permute-start.5 = (bf16[128,128]{1,0:T(8,128)(2,1)S(1)}, bf16[128,128]{1,0:T(8,128)(2,1)S(1)}, u32[]{:S(2)}, u32[]{:S(2)}) collective-permute-start(bf16[128,128]{1,0:T(8,128)(2,1)S(1)} %get-tuple-element.1604), channel_id=1, source_target_pairs={{0,2},{2,4},{4,6},{6,8},{8,10},{10,12},{12,14},{14,16},{16,18},{18... | collective-permute-start | bytes 98312 | tf_op jit(solution)/shard_map/while/body/eval_jaxpr/ppermute | solution.py:26
  553.5 6.4 %collective-permute-start.4 = (bf16[128,128]{1,0:T(8,128)(2,1)S(1)}, bf16[128,128]{1,0:T(8,128)(2,1)S(1)}, u32[]{:S(2)}, u32[]{:S(2)}) collective-permute-start(bf16[128,128]{1,0:T(8,128)(2,1)S(1)} %get-tuple-element.1603), channel_id=1, source_target_pairs={{0,2},{2,4},{4,6},{6,8},{8,10},{10,12},{12,14},{14,16},{16,18},{18... | collective-permute-start | bytes 98312 | tf_op jit(solution)/shard_map/while/body/eval_jaxpr/ppermute | solution.py:26
  560.5 6.8 %collective-permute-start.5 = (bf16[128,128]{1,0:T(8,128)(2,1)S(1)}, bf16[128,128]{1,0:T(8,128)(2,1)S(1)}, u32[]{:S(2)}, u32[]{:S(2)}) collective-permute-start(bf16[128,128]{1,0:T(8,128)(2,1)S(1)} %get-tuple-element.1604), channel_id=1, source_target_pairs={{0,2},{2,4},{4,6},{6,8},{8,10},{10,12},{12,14},{14,16},{16,18},{18... | collective-permute-start | bytes 98312 | tf_op jit(solution)/shard_map/while/body/eval_jaxpr/ppermute | solution.py:26
  560.5 6.4 %collective-permute-start.4 = (bf16[128,128]{1,0:T(8,128)(2,1)S(1)}, bf16[128,128]{1,0:T(8,128)(2,1)S(1)}, u32[]{:S(2)}, u32[]{:S(2)}) collective-permute-start(bf16[128,128]{1,0:T(8,128)(2,1)S(1)} %get-tuple-element.1603), channel_id=1, source_target_pairs={{0,2},{2,4},{4,6},{6,8},{8,10},{10,12},{12,14},{14,16},{16,18},{18... | collective-permute-start | bytes 98312 | tf_op jit(solution)/shard_map/while/body/eval_jaxpr/ppermute | solution.py:26
  567.5 6.8 %collective-permute-start.5 = (bf16[128,128]{1,0:T(8,128)(2,1)S(1)}, bf16[128,128]{1,0:T(8,128)(2,1)S(1)}, u32[]{:S(2)}, u32[]{:S(2)}) collective-permute-start(bf16[128,128]{1,0:T(8,128)(2,1)S(1)} %get-tuple-element.1604), channel_id=1, source_target_pairs={{0,2},{2,4},{4,6},{6,8},{8,10},{10,12},{12,14},{14,16},{16,18},{18... | collective-permute-start | bytes 98312 | tf_op jit(solution)/shard_map/while/body/eval_jaxpr/ppermute | solution.py:26
  567.6 6.4 %collective-permute-start.4 = (bf16[128,128]{1,0:T(8,128)(2,1)S(1)}, bf16[128,128]{1,0:T(8,128)(2,1)S(1)}, u32[]{:S(2)}, u32[]{:S(2)}) collective-permute-start(bf16[128,128]{1,0:T(8,128)(2,1)S(1)} %get-tuple-element.1603), channel_id=1, source_target_pairs={{0,2},{2,4},{4,6},{6,8},{8,10},{10,12},{12,14},{14,16},{16,18},{18... | collective-permute-start | bytes 98312 | tf_op jit(solution)/shard_map/while/body/eval_jaxpr/ppermute | solution.py:26
  574.6 6.8 %collective-permute-start.5 = (bf16[128,128]{1,0:T(8,128)(2,1)S(1)}, bf16[128,128]{1,0:T(8,128)(2,1)S(1)}, u32[]{:S(2)}, u32[]{:S(2)}) collective-permute-start(bf16[128,128]{1,0:T(8,128)(2,1)S(1)} %get-tuple-element.1604), channel_id=1, source_target_pairs={{0,2},{2,4},{4,6},{6,8},{8,10},{10,12},{12,14},{14,16},{16,18},{18... | collective-permute-start | bytes 98312 | tf_op jit(solution)/shard_map/while/body/eval_jaxpr/ppermute | solution.py:26
  574.7 6.4 %collective-permute-start.4 = (bf16[128,128]{1,0:T(8,128)(2,1)S(1)}, bf16[128,128]{1,0:T(8,128)(2,1)S(1)}, u32[]{:S(2)}, u32[]{:S(2)}) collective-permute-start(bf16[128,128]{1,0:T(8,128)(2,1)S(1)} %get-tuple-element.1603), channel_id=1, source_target_pairs={{0,2},{2,4},{4,6},{6,8},{8,10},{10,12},{12,14},{14,16},{16,18},{18... | collective-permute-start | bytes 98312 | tf_op jit(solution)/shard_map/while/body/eval_jaxpr/ppermute | solution.py:26
  581.7 6.8 %collective-permute-start.5 = (bf16[128,128]{1,0:T(8,128)(2,1)S(1)}, bf16[128,128]{1,0:T(8,128)(2,1)S(1)}, u32[]{:S(2)}, u32[]{:S(2)}) collective-permute-start(bf16[128,128]{1,0:T(8,128)(2,1)S(1)} %get-tuple-element.1604), channel_id=1, source_target_pairs={{0,2},{2,4},{4,6},{6,8},{8,10},{10,12},{12,14},{14,16},{16,18},{18... | collective-permute-start | bytes 98312 | tf_op jit(solution)/shard_map/while/body/eval_jaxpr/ppermute | solution.py:26
  581.7 6.4 %collective-permute-start.4 = (bf16[128,128]{1,0:T(8,128)(2,1)S(1)}, bf16[128,128]{1,0:T(8,128)(2,1)S(1)}, u32[]{:S(2)}, u32[]{:S(2)}) collective-permute-start(bf16[128,128]{1,0:T(8,128)(2,1)S(1)} %get-tuple-element.1603), channel_id=1, source_target_pairs={{0,2},{2,4},{4,6},{6,8},{8,10},{10,12},{12,14},{14,16},{16,18},{18... | collective-permute-start | bytes 98312 | tf_op jit(solution)/shard_map/while/body/eval_jaxpr/ppermute | solution.py:26
  588.7 6.8 %collective-permute-start.5 = (bf16[128,128]{1,0:T(8,128)(2,1)S(1)}, bf16[128,128]{1,0:T(8,128)(2,1)S(1)}, u32[]{:S(2)}, u32[]{:S(2)}) collective-permute-start(bf16[128,128]{1,0:T(8,128)(2,1)S(1)} %get-tuple-element.1604), channel_id=1, source_target_pairs={{0,2},{2,4},{4,6},{6,8},{8,10},{10,12},{12,14},{14,16},{16,18},{18... | collective-permute-start | bytes 98312 | tf_op jit(solution)/shard_map/while/body/eval_jaxpr/ppermute | solution.py:26
  588.8 6.4 %collective-permute-start.4 = (bf16[128,128]{1,0:T(8,128)(2,1)S(1)}, bf16[128,128]{1,0:T(8,128)(2,1)S(1)}, u32[]{:S(2)}, u32[]{:S(2)}) collective-permute-start(bf16[128,128]{1,0:T(8,128)(2,1)S(1)} %get-tuple-element.1603), channel_id=1, source_target_pairs={{0,2},{2,4},{4,6},{6,8},{8,10},{10,12},{12,14},{14,16},{16,18},{18... | collective-permute-start | bytes 98312 | tf_op jit(solution)/shard_map/while/body/eval_jaxpr/ppermute | solution.py:26
  595.8 6.8 %collective-permute-start.5 = (bf16[128,128]{1,0:T(8,128)(2,1)S(1)}, bf16[128,128]{1,0:T(8,128)(2,1)S(1)}, u32[]{:S(2)}, u32[]{:S(2)}) collective-permute-start(bf16[128,128]{1,0:T(8,128)(2,1)S(1)} %get-tuple-element.1604), channel_id=1, source_target_pairs={{0,2},{2,4},{4,6},{6,8},{8,10},{10,12},{12,14},{14,16},{16,18},{18... | collective-permute-start | bytes 98312 | tf_op jit(solution)/shard_map/while/body/eval_jaxpr/ppermute | solution.py:26
  595.9 6.4 %collective-permute-start.4 = (bf16[128,128]{1,0:T(8,128)(2,1)S(1)}, bf16[128,128]{1,0:T(8,128)(2,1)S(1)}, u32[]{:S(2)}, u32[]{:S(2)}) collective-permute-start(bf16[128,128]{1,0:T(8,128)(2,1)S(1)} %get-tuple-element.1603), channel_id=1, source_target_pairs={{0,2},{2,4},{4,6},{6,8},{8,10},{10,12},{12,14},{14,16},{16,18},{18... | collective-permute-start | bytes 98312 | tf_op jit(solution)/shard_map/while/body/eval_jaxpr/ppermute | solution.py:26
  (35 other events, 708.3 us)
Sparse Core Ops, SparseCore 0:
  12.1 14.4 reduce-scatter.1
where the time goes:
time: 611 us; the launch traced here: 610 us
  waiting for transfers between devices  468 us (77%)
  blocking collectives  79.3 us (13%)
  matrix products  24 us (4%)
  between operations  13.8 us (2%)
  other arithmetic  9.93 us (2%)
    ppermute x90, waiting for transfers between devices, passed_along(): return lax.ppermute(value, axis, pairs)  453 us
    all_gather x4, blocking collectives, combined_all(): pieces = jax.tree.map(lambda part: lax.all_gather(part, axis), value)  79.3 us
    dot_general x76, matrix products, score_block(): jnp.einsum('hqd,kd->hqk', query_heads, key_block, preferred_element_type=...  15.6 us
    reduce_scatter x1, waiting for transfers between devices, on_device(): lax.psum_scatter(lax.dot_general(kv_weight, tokens, (((0,), (1,)), ((), (...  14.3 us
  transfers between devices with their start and end apart: 91, of which 76 were waited for; matrix products, arithmetic and copies ran while one was open for 1% of the time, Pallas kernels for 0%

commit v1 on v0

v1 whole, which is shorter than its diff:
```python
import functools
import math

import jax
import jax.numpy as jnp
from jax import lax
from jax.experimental import pallas as pl
from jax.experimental.pallas import tpu as pltpu
from jax.sharding import PartitionSpec as P

ITERS = 2
ROPE_BASE = 500000.0
LOG2E = 1.0 / math.log(2.0)
MESH = pl.DeviceIdType.MESH
CHUNKS = 4
ROWS = 64
LINE, ACROSS, CORE, CORNER = 0, 1, 2, 3


def xor(index, mask):
    bit = 1
    while bit <= mask:
        if mask & bit:
            index = index + bit - 2 * bit * ((index // bit) % 2)
        bit *= 2
    return index


def kernel(
    ctx_size, fsdp_size, quad,
    tok_hbm, w_hbm, q_hbm, rel_ref, out_ref,
    tok, w, q, keys, values, part_out, part_in, scores, rowp, colmax, colsum, colpot, lse, heads, landed,
    load_sem, q_local, q_send, q_recv, p_send, p_recv, b_send, b_recv, l_send, l_recv, o_send, o_recv,
):
    me = lax.axis_index("ctx")
    mf = lax.axis_index("fsdp")
    groups = ctx_size // quad
    z, m = me // quad, me % quad
    rows, depth = tok.shape
    hd = q.shape[-1]
    span = quad * rows
    step = depth // CHUNKS

    def at(index):
        return (index, mf)

    loads = {}
    for order, off in enumerate(list(range(1, fsdp_size)) + [0]):
        slot = pl.multiple_of(((mf + off) % fsdp_size) * 2 * hd, 2 * hd)
        for c in range(CHUNKS):
            piece = pl.ds(c * step, step)
            if order == 0:
                loads["t", c] = pltpu.make_async_copy(tok_hbm.at[:, piece], tok.at[:, piece], load_sem.at[fsdp_size, c])
                loads["t", c].start()
            loads[off, c] = pltpu.make_async_copy(
                w_hbm.at[piece, pl.ds(slot, 2 * hd)], w.at[off, piece], load_sem.at[off, c]
            )
            loads[off, c].start()

    barrier = pltpu.get_barrier_semaphore()
    peers = [(me, (mf + off) % fsdp_size) for off in range(1, fsdp_size)]
    peers += [at(xor(z, k) * quad + m) for k in range(1, groups)]
    peers += [at(z * quad + xor(m, k)) for k in range(1, quad)]
    for peer in peers:
        pl.semaphore_signal(barrier, inc=1, device_id=peer, device_id_type=MESH)

    lane = lax.broadcasted_iota(jnp.int32, (rows, hd), 1)
    position = (me * rows + lax.broadcasted_iota(jnp.int32, (rows, hd), 0)).astype(jnp.float32)
    turn = jnp.exp((lane % (hd // 2)).astype(jnp.float32) * (-2.0 * math.log(ROPE_BASE) / hd))
    angle = position * turn
    cosine = jnp.cos(angle)
    sine = jnp.sin(angle)
    sine = jnp.where(lane < hd // 2, -sine, sine)

    pl.semaphore_wait(barrier, len(peers))

    own_q = pltpu.make_async_copy(q_hbm.at[:, pl.ds(pl.multiple_of(m * hd, hd), hd)], q.at[0], q_local)
    own_q.start()
    q_copies = []
    for k in range(1, quad):
        peer = xor(m, k)
        q_copies.append(pltpu.make_async_remote_copy(
            src_ref=q_hbm.at[:, pl.ds(pl.multiple_of(peer * hd, hd), hd)], dst_ref=q.at[k],
            send_sem=q_send.at[k], recv_sem=q_recv.at[k], device_id=at(z * quad + peer), device_id_type=MESH,
        ))
        q_copies[-1].start()

    def project(off, first):
        total = jnp.zeros((rows, 2 * hd), jnp.float32)
        for c in range(CHUNKS):
            if first:
                loads["t", c].wait()
            loads[off, c].wait()
            piece = pl.ds(c * step, step)
            total = total + jnp.dot(tok[:, piece], w[off, piece], preferred_element_type=jnp.float32)
        return total

    p_copies = {}
    for off in range(1, fsdp_size):
        total = project(off, off == 1)
        for half in range(2):
            part_out[off - 1, half] = total[:, half * hd:(half + 1) * hd]
            p_copies[off, half] = pltpu.make_async_remote_copy(
                src_ref=part_out.at[off - 1, half], dst_ref=part_in.at[off - 1, half],
                send_sem=p_send.at[off - 1, half], recv_sem=p_recv.at[off - 1, half],
                device_id=(me, (mf + off) % fsdp_size), device_id_type=MESH,
            )
            p_copies[off, half].start()
    own = project(0, fsdp_size == 1)

    def summed(half):
        total = own[:, half * hd:(half + 1) * hd]
        for off in range(1, fsdp_size):
            p_copies[off, half].wait_recv()
            total = total + part_in[off - 1, half]
        return total

    sent = []

    def ship(buffer, which, way, k, block, target):
        copy = pltpu.make_async_remote_copy(
            src_ref=buffer.at[block], dst_ref=buffer.at[block],
            send_sem=b_send.at[which, way, k], recv_sem=b_recv.at[which, way, k],
            device_id=at(target), device_id_type=MESH,
        )
        copy.start()
        sent.append(copy)

    def arrive(buffer, which, way, k, member):
        block = xor(z, k) * quad + member
        pltpu.make_async_remote_copy(
            src_ref=buffer.at[block], dst_ref=buffer.at[block],
            send_sem=b_send.at[which, way, k], recv_sem=b_recv.at[which, way, k],
            device_id=at(block), device_id_type=MESH,
        ).wait_recv()
        return block

    core, across = z * quad + xor(m, 1), z * quad + xor(m, 2)

    def launch(buffer, which):
        for k in range(groups - 1, 0, -1):
            ship(buffer, which, LINE, k, me, xor(z, k) * quad + m)
        ship(buffer, which, ACROSS, 0, me, across)
        ship(buffer, which, CORE, 0, me, core)

    def from_line(buffer, which, k):
        block = arrive(buffer, which, LINE, k, m)
        ship(buffer, which, ACROSS, k, block, across)
        ship(buffer, which, CORE, k, block, core)

    def from_across(buffer, which, k):
        block = arrive(buffer, which, ACROSS, k, xor(m, 2))
        ship(buffer, which, CORNER, k, block, core)

    def complete(buffer, which, k):
        arrive(buffer, which, CORE, k, xor(m, 1))
        arrive(buffer, which, CORNER, k, xor(m, 3))

    key_part = summed(0)
    keys[me] = (key_part * cosine + pltpu.roll(key_part, hd // 2, 1) * sine).astype(jnp.bfloat16)
    launch(keys, 0)
    values[me] = summed(1).astype(jnp.bfloat16)
    own_q.wait()
    for copy in q_copies:
        copy.wait_recv()

    scale = LOG2E / math.sqrt(hd)

    def score_group(k):
        first = xor(z, k)
        block = keys[pl.ds(first * quad, quad)].reshape(span, hd)
        for part in range(quad):
            piece = lax.dot_general(q[part], block, (((1,), (1,)), ((), ())), preferred_element_type=jnp.float32)
            scores[pl.ds(part * rows, rows), pl.ds(pl.multiple_of(first * span, span), span)] = piece * scale

    for k in range(1, groups):
        from_line(keys, 0, k)
        from_across(keys, 0, k - 1)
    launch(values, 1)
    for k in range(groups - 1):
        complete(keys, 0, k)
        score_group(k)
    from_across(keys, 0, groups - 1)
    complete(keys, 0, groups - 1)
    score_group(groups - 1)

    rate = rel_ref[m]
    seq = scores.shape[1]
    blocks = span // ROWS

    def shifted(part, first):
        block = scores[part, :]
        if first:
            return block
        return (block.reshape(ROWS // 8, 8, seq) + colpot[...][None]).reshape(ROWS, seq)

    for it in range(ITERS):
        colmax[...] = jnp.full_like(colmax, -jnp.inf)

        @pl.loop(0, blocks)
        def _(i):
            part = pl.ds(pl.multiple_of(i * ROWS, ROWS), ROWS)
            peak = jnp.max(shifted(part, it == 0), axis=1, keepdims=True)
            mass = jnp.sum(jnp.exp2(shifted(part, it == 0) - peak), axis=1, keepdims=True)
            pot = -rate * (peak + jnp.log2(mass))
            rowp[part, :] = pot
            colmax[...] = jnp.maximum(colmax[...], jnp.max((scores[part, :] + pot).reshape(ROWS // 8, 8, seq), axis=0))

        top = jnp.max(colmax[...], axis=0, keepdims=True)
        colsum[...] = jnp.zeros_like(colsum)
        colmax[...] = jnp.broadcast_to(top, colmax.shape)

        @pl.loop(0, blocks)
        def _(i):
            part = pl.ds(pl.multiple_of(i * ROWS, ROWS), ROWS)
            lifted = (scores[part, :] + rowp[part, :]).reshape(ROWS // 8, 8, seq) - colmax[...][None]
            colsum[...] += jnp.sum(jnp.exp2(lifted), axis=0)

        lse[it, z] = top + jnp.log2(jnp.sum(colsum[...], axis=0, keepdims=True))
        for k in range(groups - 1, 0, -1):
            copy = pltpu.make_async_remote_copy(
                src_ref=lse.at[it, z], dst_ref=lse.at[it, z], send_sem=l_send.at[it, k], recv_sem=l_recv.at[it, k],
                device_id=at(xor(z, k) * quad + m), device_id_type=MESH,
            )
            copy.start()
            sent.append(copy)
        if it == 0:
            for k in range(1, groups):
                from_line(values, 1, k)
        if it == ITERS - 1:
            for k in range(groups):
                from_across(values, 1, k)
        for k in range(1, groups):
            other = xor(z, k)
            pltpu.make_async_remote_copy(
                src_ref=lse.at[it, other], dst_ref=lse.at[it, other], send_sem=l_send.at[it, k],
                recv_sem=l_recv.at[it, k], device_id=at(other * quad + m), device_id_type=MESH,
            ).wait_recv()
        terms = [lse[it, g] for g in range(groups)]
        top = functools.reduce(jnp.maximum, terms)
        mass = functools.reduce(jnp.add, [jnp.exp2(term - top) for term in terms])
        colpot[...] = jnp.broadcast_to(-rate * (top + jnp.log2(mass)), colpot.shape)

    for k in range(groups):
        complete(values, 1, k)
    value_rows = values[...].reshape(seq, hd)

    o_copies = []
    for k in range(quad - 1, -1, -1):
        numer = []
        for half in range(rows // ROWS):
            part = pl.ds(k * rows + half * ROWS, ROWS)
            peak = jnp.max(shifted(part, False), axis=1, keepdims=True)
            weights = jnp.exp2(shifted(part, False) - peak)
            total = jnp.sum(weights, axis=1, keepdims=True)
            blended = jnp.dot(weights.astype(jnp.bfloat16), value_rows, preferred_element_type=jnp.float32)
            heads[k, pl.ds(half * ROWS, ROWS), :] = (blended / total).astype(jnp.bfloat16)
        if k:
            o_copies.append(pltpu.make_async_remote_copy(
                src_ref=heads.at[k], dst_ref=landed.at[k], send_sem=o_send.at[k], recv_sem=o_recv.at[k],
                device_id=at(z * quad + xor(m, k)), device_id_type=MESH,
            ))
            o_copies[-1].start()
    out_ref[:, pl.ds(pl.multiple_of(m * hd, hd), hd)] = heads[0]
    for k, copy in zip(range(quad - 1, 0, -1), o_copies):
        copy.wait_recv()
        out_ref[:, pl.ds(pl.multiple_of(xor(m, k) * hd, hd), hd)] = landed[k]
    for copy in q_copies + list(p_copies.values()) + sent + o_copies:
        copy.wait_send()


def on_device(ctx_size, fsdp_size, tokens, kv_weight, queries, relaxation):
    rows, depth = tokens.shape
    quad = relaxation.shape[0]
    groups = ctx_size // quad
    hd = kv_weight.shape[1] // fsdp_size // 2
    seq = ctx_size * rows
    bf16, f32 = jnp.bfloat16, jnp.float32
    dma = pltpu.SemaphoreType.DMA
    others = max(fsdp_size - 1, 1)
    return pl.pallas_call(
        functools.partial(kernel, ctx_size, fsdp_size, quad),
        out_shape=jax.ShapeDtypeStruct(queries.shape, bf16),
        in_specs=[pl.BlockSpec(memory_space=pl.ANY)] * 3 + [pl.BlockSpec(memory_space=pltpu.SMEM)],
        out_specs=pl.BlockSpec(memory_space=pltpu.VMEM),
        scratch_shapes=[
            pltpu.VMEM((rows, depth), bf16),
            pltpu.VMEM((fsdp_size, depth, 2 * hd), bf16),
            pltpu.VMEM((quad, rows, hd), bf16),
            pltpu.VMEM((ctx_size, rows, hd), bf16),
            pltpu.VMEM((ctx_size, rows, hd), bf16),
            pltpu.VMEM((others, 2, rows, hd), f32),
            pltpu.VMEM((others, 2, rows, hd), f32),
            pltpu.VMEM((quad * rows, seq), f32),
            pltpu.VMEM((quad * rows, 1), f32),
            pltpu.VMEM((8, seq), f32),
            pltpu.VMEM((8, seq), f32),
            pltpu.VMEM((8, seq), f32),
            pltpu.VMEM((ITERS, groups, 1, seq), f32),
            pltpu.VMEM((quad, rows, hd), bf16),
            pltpu.VMEM((quad, rows, hd), bf16),
            dma((fsdp_size + 1, CHUNKS)),
            dma,
            dma((quad,)), dma((quad,)),
            dma((others, 2)), dma((others, 2)),
            dma((2, 4, groups)), dma((2, 4, groups)),
            dma((ITERS, groups)), dma((ITERS, groups)),
            dma((quad,)), dma((quad,)),
        ],
        compiler_params=pltpu.CompilerParams(
            collective_id=0, has_side_effects=True, vmem_limit_bytes=60 * 1024 * 1024
        ),
    )(tokens, kv_weight, queries, relaxation)


def solution(mesh):
    placed = (P("ctx", "fsdp"), P("fsdp", None), P("ctx", "fsdp"), P("fsdp"))
    body = functools.partial(on_device, mesh.shape["ctx"], mesh.shape["fsdp"])
    return jax.shard_map(body, mesh=mesh, in_specs=placed, out_specs=P("ctx", "fsdp"), check_vma=False)
```

time: 611 us -> 41.7 us (0.07)
  waiting for transfers between devices: 468 us -> 0 us
  blocking collectives: 79.3 us -> 0 us
  Pallas kernels: 0 us -> 40 us
  matrix products: 24 us -> 0 us
  between operations: 13.8 us -> 0.01 us
  other arithmetic: 9.93 us -> 0 us
    ppermute x90 -> x0, waiting for transfers between devices: 453 us -> none  [passed_along(): return lax.ppermute(value, axis, pairs)]
    all_gather x4 -> x0, blocking collectives: 79.3 us -> none  [combined_all(): pieces = jax.tree.map(lambda part: lax.all_gather(part, axis), value)]
    pallas_call x0 -> x1, Pallas kernels: none -> 40 us  [on_device(): pl.pallas_call(functools.partial(kernel, ctx_size, fsdp_size, quad), out_...]
    dot_general x93 -> x0, matrix products: 24 us -> none  [the longest x76 15.6 us: score_block(): jnp.einsum('hqd,kd->hqk', query_heads, key_block, preferred_element_type=...]
    reduce_scatter x1 -> x0, waiting for transfers between devices: 14.3 us -> none  [on_device(): lax.psum_scatter(lax.dot_general(kv_weight, tokens, (((0,), (1,)), ((), (...]
  transfers between devices with their start and end apart: 91 -> 0, of which waited for: 76 -> 0; matrix products, arithmetic and copies ran while one was open for 1% -> 0% of each run, Pallas kernels for 0% -> 0%
where the time goes in v1:
time: 41.7 us; the launch traced here: 41.5 us
  Pallas kernels  40 us (96%)
  local copies, waits for them, and re-layouts  1.57 us (4%)
    pallas_call x1, Pallas kernels, on_device(): pl.pallas_call(functools.partial(kernel, ctx_size, fsdp_size, quad), out_...  40 us
    unnamed x1, local copies, waits for them, and re-layouts  1.57 us

profile of v1, /device:TPU:0, one launch (start us, length us, event | category | flops | bytes accessed | tf_op | source)
XLA Modules:
  0.0 41.5 jit_solution(5944709952646000805)
XLA Ops:
  0.0 40.0 %shard_map.46 = bf16[128,512]{1,0:T(8,128)(2,1)} custom-call(bf16[128,4096]{1,0:T(8,128)(2,1)} %tok_hbm.1, bf16[4096,512]{1,0:T(8,128)(2,1)} %w_hbm.1, bf16[128,512]{1,0:T(8,128)(2,1)} %q_hbm.1, f32[4]{0:T(128)} %rel_ref.1), custom_call_target="tpu_custom_call" | custom-call | tf_op jit(solution)/shard_map/pallas_call | solution.py:281
  40.0 1.6 %copy.6 = bf16[128,512]{1,0:T(8,128)(2,1)} copy(bf16[128,512]{1,0:T(8,128)(2,1)} %shard_map.46) | data formatting | bytes 262144

commit v2 on v1

--- a/solution.py
+++ b/solution.py
@@ -13,7 +13,8 @@
 LOG2E = 1.0 / math.log(2.0)
 MESH = pl.DeviceIdType.MESH
 CHUNKS = 4
-ROWS = 64
+ROWS = 128
+OUT_ROWS = 64
 LINE, ACROSS, CORE, CORNER = 0, 1, 2, 3
 
 
@@ -72,7 +73,33 @@
     sine = jnp.sin(angle)
     sine = jnp.where(lane < hd // 2, -sine, sine)
 
+    def project(off, first):
+        total = jnp.zeros((rows, 2 * hd), jnp.float32)
+        for c in range(CHUNKS):
+            if first:
+                loads["t", c].wait()
+            loads[off, c].wait()
+            piece = pl.ds(c * step, step)
+            total = total + jnp.dot(tok[:, piece], w[off, piece], preferred_element_type=jnp.float32)
+        return total
+
+    totals = [project(off, off == 1) for off in range(1, fsdp_size)]
+    own = project(0, fsdp_size == 1)
+    for off in range(1, fsdp_size):
+        for half in range(2):
+            part_out[off - 1, half] = totals[off - 1][:, half * hd:(half + 1) * hd]
+
     pl.semaphore_wait(barrier, len(peers))
+
+    p_copies = {}
+    for half in range(2):
+        for off in range(1, fsdp_size):
+            p_copies[off, half] = pltpu.make_async_remote_copy(
+                src_ref=part_out.at[off - 1, half], dst_ref=part_in.at[off - 1, half],
+                send_sem=p_send.at[off - 1, half], recv_sem=p_recv.at[off - 1, half],
+                device_id=(me, (mf + off) % fsdp_size), device_id_type=MESH,
+            )
+            p_copies[off, half].start()
 
     own_q = pltpu.make_async_copy(q_hbm.at[:, pl.ds(pl.multiple_of(m * hd, hd), hd)], q.at[0], q_local)
     own_q.start()
@@ -85,29 +112,6 @@
         ))
         q_copies[-1].start()
 
-    def project(off, first):
-        total = jnp.zeros((rows, 2 * hd), jnp.float32)
-        for c in range(CHUNKS):
-            if first:
-                loads["t", c].wait()
-            loads[off, c].wait()
-            piece = pl.ds(c * step, step)
-            total = total + jnp.dot(tok[:, piece], w[off, piece], preferred_element_type=jnp.float32)
-        return total
-
-    p_copies = {}
-    for off in range(1, fsdp_size):
-        total = project(off, off == 1)
-        for half in range(2):
-            part_out[off - 1, half] = total[:, half * hd:(half + 1) * hd]
-            p_copies[off, half] = pltpu.make_async_remote_copy(
-                src_ref=part_out.at[off - 1, half], dst_ref=part_in.at[off - 1, half],
-                send_sem=p_send.at[off - 1, half], recv_sem=p_recv.at[off - 1, half],
-                device_id=(me, (mf + off) % fsdp_size), device_id_type=MESH,
-            )
-            p_copies[off, half].start()
-    own = project(0, fsdp_size == 1)
-
     def summed(half):
         total = own[:, half * hd:(half + 1) * hd]
         for off in range(1, fsdp_size):
@@ -192,7 +196,7 @@
         block = scores[part, :]
         if first:
             return block
-        return (block.reshape(ROWS // 8, 8, seq) + colpot[...][None]).reshape(ROWS, seq)
+        return (block.reshape(-1, 8, seq) + colpot[...][None]).reshape(block.shape)
 
     for it in range(ITERS):
         colmax[...] = jnp.full_like(colmax, -jnp.inf)
@@ -247,14 +251,13 @@
 
     o_copies = []
     for k in range(quad - 1, -1, -1):
-        numer = []
-        for half in range(rows // ROWS):
-            part = pl.ds(k * rows + half * ROWS, ROWS)
+        for half in range(rows // OUT_ROWS):
+            part = pl.ds(k * rows + half * OUT_ROWS, OUT_ROWS)
             peak = jnp.max(shifted(part, False), axis=1, keepdims=True)
             weights = jnp.exp2(shifted(part, False) - peak)
             total = jnp.sum(weights, axis=1, keepdims=True)
             blended = jnp.dot(weights.astype(jnp.bfloat16), value_rows, preferred_element_type=jnp.float32)
-            heads[k, pl.ds(half * ROWS, ROWS), :] = (blended / total).astype(jnp.bfloat16)
+            heads[k, pl.ds(half * OUT_ROWS, OUT_ROWS), :] = (blended / total).astype(jnp.bfloat16)
         if k:
             o_copies.append(pltpu.make_async_remote_copy(
                 src_ref=heads.at[k], dst_ref=landed.at[k], send_sem=o_send.at[k], recv_sem=o_recv.at[k],
@@ -278,6 +281,7 @@
     bf16, f32 = jnp.bfloat16, jnp.float32
     dma = pltpu.SemaphoreType.DMA
     others = max(fsdp_size - 1, 1)
+    in_hbm = [pltpu.with_memory_space_constraint(a, pltpu.HBM) for a in (tokens, kv_weight, queries, relaxation)]
     return pl.pallas_call(
         functools.partial(kernel, ctx_size, fsdp_size, quad),
         out_shape=jax.ShapeDtypeStruct(queries.shape, bf16),
@@ -308,9 +312,9 @@
             dma((quad,)), dma((quad,)),
         ],
         compiler_params=pltpu.CompilerParams(
-            collective_id=0, has_side_effects=True, vmem_limit_bytes=60 * 1024 * 1024
+            collective_id=0, has_side_effects=True, vmem_limit_bytes=52 * 1024 * 1024
         ),
-    )(tokens, kv_weight, queries, relaxation)
+    )(*in_hbm)
 
 
 def solution(mesh):

time: 41.7 us -> 38 us (0.911)
  Pallas kernels: 40 us -> 37.1 us
  local copies, waits for them, and re-layouts: 1.57 us -> 0.66 us
    pallas_call x1, Pallas kernels: 40 us -> 37.1 us  [on_device(): pl.pallas_call(functools.partial(kernel, ctx_size, fsdp_size, quad), out_...]
    unnamed x1, local copies, waits for them, and re-layouts: 1.57 us -> 0.66 us
where the time goes in v2:
time: 38 us; the launch traced here: 37.8 us
  Pallas kernels  37.1 us (98%)
  local copies, waits for them, and re-layouts  0.66 us (2%)
    pallas_call x1, Pallas kernels, on_device(): pl.pallas_call(functools.partial(kernel, ctx_size, fsdp_size, quad), out_...  37.1 us

profile of v2, /device:TPU:0, one launch (start us, length us, event | category | flops | bytes accessed | tf_op | source)
XLA Modules:
  0.0 37.8 jit_solution(5335073173998260906)
XLA Ops:
  0.0 37.1 %shard_map.46 = bf16[128,512]{1,0:T(8,128)(2,1)S(1)} custom-call(bf16[128,4096]{1,0:T(8,128)(2,1)} %tok_hbm.1, bf16[4096,512]{1,0:T(8,128)(2,1)} %w_hbm.1, bf16[128,512]{1,0:T(8,128)(2,1)} %q_hbm.1, f32[4]{0:T(128)} %rel_ref.1), custom_call_target="tpu_custom_call" | custom-call | tf_op jit(solution)/shard_map/pallas_call | solution.py:285
  37.1 0.7 %copy.6 = bf16[128,512]{1,0:T(8,128)(2,1)} copy(bf16[128,512]{1,0:T(8,128)(2,1)S(1)} %shard_map.46) | data formatting | bytes 262144

commit v3 on v2

--- a/solution.py
+++ b/solution.py
@@ -13,9 +13,12 @@
 LOG2E = 1.0 / math.log(2.0)
 MESH = pl.DeviceIdType.MESH
 CHUNKS = 4
-ROWS = 128
+ROWS = 256
 OUT_ROWS = 64
 LINE, ACROSS, CORE, CORNER = 0, 1, 2, 3
+
+
+DIRECT = (2, 3)
 
 
 def xor(index, mask):
@@ -30,7 +33,7 @@
 def kernel(
     ctx_size, fsdp_size, quad,
     tok_hbm, w_hbm, q_hbm, rel_ref, out_ref,
-    tok, w, q, keys, values, part_out, part_in, scores, rowp, colmax, colsum, colpot, lse, heads, landed,
+    tok, w, q, keys, values, part_out, part_in, scores, peaks, rowp, colmax, colsum, colpot, lse, heads, landed,
     load_sem, q_local, q_send, q_recv, p_send, p_recv, b_send, b_recv, l_send, l_recv, o_send, o_recv,
 ):
     me = lax.axis_index("ctx")
@@ -62,6 +65,8 @@
     peers = [(me, (mf + off) % fsdp_size) for off in range(1, fsdp_size)]
     peers += [at(xor(z, k) * quad + m) for k in range(1, groups)]
     peers += [at(z * quad + xor(m, k)) for k in range(1, quad)]
+    direct = [k for k in DIRECT if k < groups]
+    peers += [at(xor(z, k) * quad + xor(m, 2)) for k in direct]
     for peer in peers:
         pl.semaphore_signal(barrier, inc=1, device_id=peer, device_id_type=MESH)
 
@@ -144,12 +149,16 @@
     def launch(buffer, which):
         for k in range(groups - 1, 0, -1):
             ship(buffer, which, LINE, k, me, xor(z, k) * quad + m)
+        if which == 0:
+            for k in direct:
+                ship(buffer, which, ACROSS, k, me, xor(z, k) * quad + xor(m, 2))
         ship(buffer, which, ACROSS, 0, me, across)
         ship(buffer, which, CORE, 0, me, core)
 
     def from_line(buffer, which, k):
         block = arrive(buffer, which, LINE, k, m)
-        ship(buffer, which, ACROSS, k, block, across)
+        if which == 1 or k not in direct:
+            ship(buffer, which, ACROSS, k, block, across)
         ship(buffer, which, CORE, k, block, core)
 
     def from_across(buffer, which, k):
@@ -174,19 +183,23 @@
         first = xor(z, k)
         block = keys[pl.ds(first * quad, quad)].reshape(span, hd)
         for part in range(quad):
-            piece = lax.dot_general(q[part], block, (((1,), (1,)), ((), ())), preferred_element_type=jnp.float32)
-            scores[pl.ds(part * rows, rows), pl.ds(pl.multiple_of(first * span, span), span)] = piece * scale
+            piece = scale * lax.dot_general(
+                q[part], block, (((1,), (1,)), ((), ())), preferred_element_type=jnp.float32
+            )
+            place = pl.ds(part * rows, rows)
+            scores[place, pl.ds(pl.multiple_of(first * span, span), span)] = piece
+            peak = jnp.max(piece, axis=1, keepdims=True)
+            peaks[place, :] = jnp.maximum(peaks[place, :], peak) if k else peak
 
     for k in range(1, groups):
         from_line(keys, 0, k)
         from_across(keys, 0, k - 1)
     launch(values, 1)
-    for k in range(groups - 1):
+    for k in range(groups):
+        if k == max(groups - 2, 0):
+            from_across(keys, 0, groups - 1)
         complete(keys, 0, k)
         score_group(k)
-    from_across(keys, 0, groups - 1)
-    complete(keys, 0, groups - 1)
-    score_group(groups - 1)
 
     rate = rel_ref[m]
     seq = scores.shape[1]
@@ -204,7 +217,7 @@
         @pl.loop(0, blocks)
         def _(i):
             part = pl.ds(pl.multiple_of(i * ROWS, ROWS), ROWS)
-            peak = jnp.max(shifted(part, it == 0), axis=1, keepdims=True)
+            peak = jnp.max(shifted(part, False), axis=1, keepdims=True) if it else peaks[part, :]
             mass = jnp.sum(jnp.exp2(shifted(part, it == 0) - peak), axis=1, keepdims=True)
             pot = -rate * (peak + jnp.log2(mass))
             rowp[part, :] = pot
@@ -297,6 +310,7 @@
             pltpu.VMEM((others, 2, rows, hd), f32),
             pltpu.VMEM((quad * rows, seq), f32),
             pltpu.VMEM((quad * rows, 1), f32),
+            pltpu.VMEM((quad * rows, 1), f32),
             pltpu.VMEM((8, seq), f32),
             pltpu.VMEM((8, seq), f32),
             pltpu.VMEM((8, seq), f32),

time: 38 us -> 36.8 us (0.968)
  Pallas kernels: 37.1 us -> 35.9 us
    pallas_call x1, Pallas kernels: 37.1 us -> 35.9 us  [on_device(): pl.pallas_call(functools.partial(kernel, ctx_size, fsdp_size, quad), out_...]
where the time goes in v3:
time: 36.8 us; the launch traced here: 36.6 us
  Pallas kernels  35.9 us (98%)
  local copies, waits for them, and re-layouts  0.66 us (2%)
    pallas_call x1, Pallas kernels, on_device(): pl.pallas_call(functools.partial(kernel, ctx_size, fsdp_size, quad), out_...  35.9 us

profile of v3, /device:TPU:0, one launch (start us, length us, event | category | flops | bytes accessed | tf_op | source)
XLA Modules:
  0.0 36.6 jit_solution(7727380290824597401)
XLA Ops:
  0.0 35.9 %shard_map.46 = bf16[128,512]{1,0:T(8,128)(2,1)S(1)} custom-call(bf16[128,4096]{1,0:T(8,128)(2,1)} %tok_hbm.1, bf16[4096,512]{1,0:T(8,128)(2,1)} %w_hbm.1, bf16[128,512]{1,0:T(8,128)(2,1)} %q_hbm.1, f32[4]{0:T(128)} %rel_ref.1), custom_call_target="tpu_custom_call" | custom-call | tf_op jit(solution)/shard_map/pallas_call | solution.py:298
  35.9 0.7 %copy.6 = bf16[128,512]{1,0:T(8,128)(2,1)} copy(bf16[128,512]{1,0:T(8,128)(2,1)S(1)} %shard_map.46) | data formatting | bytes 262144
